TPU v7x, 512 devices: a whole 4x4x16 slice. The times are simulated.
512 devices in a mesh: wide: 64 (over y_lo, z, core), narrow: 8 (over y_hi, x).
Axes of the slice: x: 4, y: 4 (y_hi: 2, y_lo: 2; y = y_hi * 2 + y_lo), z: 16, core: 2. Of those that a mesh axis runs over, the one named last changes fastest.
Arguments:
- tokens: bfloat16 [8192, 2048], P('wide', 'narrow'), may hold values from -6 to 6
- expert_ids: int32 [8192, 6], P('wide'), may hold values from 0 to 63, all different within a row; in each aligned block of 128 rows (0 to 127, 128 to 255, ...) at most 14 rows name the same one
- route_weights: bfloat16 [8192, 6], P('wide'), may hold values from 0.049804688 to 0.5
- w_gate: bfloat16 [64, 1408, 2048], P('wide', 'narrow'), may hold values from -0.125 to 0.125
- w_up: bfloat16 [64, 1408, 2048], P('wide', 'narrow'), may hold values from -0.125 to 0.125
- w_down: bfloat16 [64, 1408, 2048], P('wide', 'narrow'), may hold values from -0.15625 to 0.15625
Outputs:
- mixed: bfloat16 [8192, 2048], P('wide', 'narrow')
Inputs may be any that keep to these rules, and one draw needn't show every extreme that they name: `expert_ids`: within a row the 6 experts differ. Among the 128 tokens of one aligned block, no expert is named more than 14 times, a bound that some block reaches.
All inputs are finite; a program needn't handle non-finite values.
Results may differ from a plain program's by a relative error of at most 0.017.
Values may be sent and summed in bfloat16 or wider, within the bound.
A program may use at most 64 MiB of HBM per device.

v0:
```python
import jax
import jax.numpy as jnp
from jax import lax
from jax.sharding import PartitionSpec as P


def local(tokens, expert_ids, route_weights, w_gate, w_up, w_down):
    tok_rows = expert_ids.shape[0]
    top_count = expert_ids.shape[1]
    local_experts = w_gate.shape[0]
    groups_wide = lax.axis_size("wide")
    experts_all = local_experts * groups_wide
    capacity = 7 * tok_rows * top_count // (6 * experts_all)
    slots_all = experts_all * capacity
    flat_ids = expert_ids.reshape(-1)
    onehot = (flat_ids[:, None] == jnp.arange(experts_all, dtype=jnp.int32)[None, :]).astype(
        jnp.int32
    )
    running = jnp.cumsum(onehot, axis=0)
    slot_index = jnp.sum(running * onehot, axis=1) - 1
    destination = (flat_ids * capacity + slot_index).reshape(tok_rows, top_count)
    hit = destination[:, :, None] == jnp.arange(slots_all, dtype=jnp.int32)[None, None, :]
    dispatch = jnp.any(hit, axis=1).astype(jnp.bfloat16)
    combine = jnp.sum(
        jnp.where(hit, route_weights.astype(jnp.float32)[:, :, None], 0.0), axis=1
    ).astype(jnp.bfloat16)
    outgoing = jnp.einsum("ts,td->sd", dispatch, tokens, preferred_element_type=jnp.float32).astype(
        jnp.bfloat16
    )
    received = lax.all_to_all(outgoing, "wide", split_axis=0, concat_axis=0, tiled=True)
    slot_rows = lax.all_gather(received, "narrow", axis=1, tiled=True)
    gate_proj = jnp.einsum("sd,fd->sf", slot_rows, w_gate[0], preferred_element_type=jnp.float32)
    up_proj = jnp.einsum("sd,fd->sf", slot_rows, w_up[0], preferred_element_type=jnp.float32)
    hidden = (jax.nn.silu(gate_proj) * up_proj).astype(jnp.bfloat16)
    partial_value = jnp.einsum(
        "sf,fd->sd", hidden, w_down[0], preferred_element_type=jnp.float32
    ).astype(jnp.bfloat16)
    summed = lax.psum_scatter(partial_value, "narrow", scatter_dimension=1, tiled=True)
    returned = lax.all_to_all(summed, "wide", split_axis=0, concat_axis=0, tiled=True)
    mixed = jnp.einsum("ts,sd->td", combine, returned, preferred_element_type=jnp.float32)
    return mixed.astype(jnp.bfloat16)


def solution(mesh):
    in_specs = (
        P("wide", "narrow"),
        P("wide", None),
        P("wide", None),
        P("wide", "narrow", None),
        P("wide", "narrow", None),
        P("wide", "narrow", None),
    )
    out_specs = P("wide", "narrow")
    return jax.shard_map(local, mesh=mesh, in_specs=in_specs, out_specs=out_specs, check_vma=False)
```

profile of v0, /device:TPU:1, one launch (start us, length us, event | category | flops | bytes accessed | tf_op | source)
XLA Modules:
  0.0 307.2 jit_solution(4234591035933541755)
XLA Ops:
  6.5 0.0 copy-start
  6.5 0.0 all-gather.2.cloned.1.call-start
  6.5 0.9 copy.21
  7.4 0.1 eq.42
  7.6 0.1 eq.38
  7.7 1.8 reduce-window.6
  9.5 0.3 slice_reduce_fusion
  9.8 0.1 fusion.15
  10.0 0.1 sub.7
  10.1 0.1 copy.24
  10.2 0.7 multiply_add_fusion
  10.9 0.4 fusion
  11.4 1.2 convolution_convert_fusion.1
  12.5 0.1 all_to_all.16
  12.7 49.6 %all_to_all.24 = bf16[64,14,256]{2,1,0:T(8,128)(2,1)S(1)} all-to-all(bf16[64,14,256]{2,1,0:T(8,128)(2,1)S(1)} %all_to_all.16), channel_id=1, replica_groups=mesh['wide'=64,'narrow'=8] {'wide'}, dimensions={0} | all-to-all | bytes 917504 | tf_op jit(solution)/shard_map/all_to_all | solution.py:30
  62.3 0.9 all_to_all.18
  63.2 0.0 all-gather.2.cloned.1.call-update
  63.3 0.0 reduce-scatter.2.cloned.1.call-start
  63.3 81.2 %all-gather.2.cloned.1.call-done = bf16[896,2048]{1,0:T(8,128)(2,1)} async-done(((bf16[896,256]{1,0:T(8,128)(2,1)}), bf16[896,2048]{1,0:T(8,128)(2,1)}) %all-gather.2.cloned.1.call-update) | async-done | bytes 3670032 | tf_op jit(solution)/shard_map/all_gather | solution.py:31
  144.5 0.0 copy-done.2
  144.5 3.4 %fusion.5 = f32[896,176]{0,1:T(8,128)S(1)} fusion(bf16[896,2048]{1,0:T(8,128)(2,1)} %all-gather.2.cloned.1.call-done, bf16[1,176,2048]{2,1,0:T(8,128)(2,1)S(1)} %copy-done.2), kind=kOutput, calls=%fused_computation.10 | convolution fusion | flops 645922816 | bytes 5021696 | tf_op jit(solution)/shard_map/sd,fd->sf/dot_general | solution.py:32
  147.9 0.0 copy-done
  147.9 0.0 copy-done.3
  147.9 6.5 %convolution_convert_fusion = bf16[896,2048]{1,0:T(8,128)(2,1)} fusion(bf16[896,2048]{1,0:T(8,128)(2,1)} %all-gather.2.cloned.1.call-done, bf16[1,176,2048]{2,1,0:T(8,128)(2,1)S(1)} %copy-done, bf16[1,176,2048]{2,1,0:T(8,128)(2,1)S(1)} %copy-done.3, f32[896,176]{0,1:T(8,128)S(1)} %fusion.5), kind=kOutput, calls=%fused_computation | convolution fusion | flops 1294626816 | bytes 9412608 | tf_op jit(solution)/shard_map/sf,fd->sd/dot_general | solution.py:35
  154.4 0.0 reduce-scatter.2.cloned.1.call-update
  154.4 96.4 %reduce-scatter.2.cloned.1.call-done = bf16[896,256]{1,0:T(8,128)(2,1)} async-done(((bf16[896,2048]{1,0:T(8,128)(2,1)}), bf16[896,256]{1,0:T(8,128)(2,1)}) %reduce-scatter.2.cloned.1.call-update) | async-done | bytes 458768 | tf_op jit(solution)/shard_map/reduce_scatter | solution.py:38
  250.8 1.9 all_to_all.19
  252.7 14.9 %all-to-all-start.1 = ((bf16[64,14,256]{2,1,0:T(8,128)(2,1)}), bf16[64,14,256]{2,1,0:T(8,128)(2,1)S(1)}, u32[]{:S(2)}, u32[]{:S(2)}) async-start(bf16[64,14,256]{2,1,0:T(8,128)(2,1)} %all_to_all.19), calls=%async_computation.2 | async-start | bytes 1048576 | tf_op jit(solution)/shard_map/all_to_all | solution.py:39
  267.7 0.3 select_reduce_fusion
  268.1 31.3 %all-to-all-done.1 = bf16[64,14,256]{2,1,0:T(8,128)(2,1)S(1)} async-done(((bf16[64,14,256]{2,1,0:T(8,128)(2,1)}), bf16[64,14,256]{2,1,0:T(8,128)(2,1)S(1)}, u32[]{:S(2)}, u32[]{:S(2)}) %all-to-all-start.1) | async-done | bytes 458784 | tf_op jit(solution)/shard_map/all_to_all | solution.py:39
  299.4 0.1 all_to_all.21
  299.5 0.9 convolution_convert_fusion.2
  (8 shorter events, 0.1 us)
Async XLA Ops:
  6.5 141.4 %copy-start = (bf16[1,176,2048]{2,1,0:T(8,128)(2,1)S(1)}, bf16[1,176,2048]{2,1,0:T(8,128)(2,1)}, u32[]{:S(2)}) copy-start(bf16[1,176,2048]{2,1,0:T(8,128)(2,1)} %param.11) | copy-start | bytes 2162692
  6.5 138.0 %copy-start.2 = (bf16[1,176,2048]{2,1,0:T(8,128)(2,1)S(1)}, bf16[1,176,2048]{2,1,0:T(8,128)(2,1)}, u32[]{:S(2)}) copy-start(bf16[1,176,2048]{2,1,0:T(8,128)(2,1)} %param.9) | copy-start | bytes 2162692
  6.5 138.0 %all-gather.2.cloned.1.call-start = ((), (), s32[]{:S(2)}) async-start(), calls=%async_computation.3 | async-start | bytes 4128768 | tf_op jit(solution)/shard_map/all_gather | solution.py:31
  62.3 85.6 %copy-start.3 = (bf16[1,176,2048]{2,1,0:T(8,128)(2,1)S(1)}, bf16[1,176,2048]{2,1,0:T(8,128)(2,1)}, u32[]{:S(2)}) copy-start(bf16[1,176,2048]{2,1,0:T(8,128)(2,1)} %param.10) | copy-start | bytes 2162692
  63.3 187.5 %reduce-scatter.2.cloned.1.call-start = ((), (), s32[]{:S(2)}) async-start(), calls=%async_computation.4 | async-start | bytes 4128768 | tf_op jit(solution)/shard_map/reduce_scatter | solution.py:38
  154.4 113.3 %copy-start.1 = (bf16[128,6]{0,1:T(8,128)(2,1)S(1)}, bf16[128,6]{0,1:T(8,128)(2,1)}, u32[]{:S(2)}) copy-start(bf16[128,6]{0,1:T(8,128)(2,1)} %param.8) | copy-start | bytes 4612
  252.7 46.6 %all-to-all-start.1 = ((bf16[64,14,256]{2,1,0:T(8,128)(2,1)}), bf16[64,14,256]{2,1,0:T(8,128)(2,1)S(1)}, u32[]{:S(2)}, u32[]{:S(2)}) async-start(bf16[64,14,256]{2,1,0:T(8,128)(2,1)} %all_to_all.19), calls=%async_computation.2 | async-start | bytes 1048576 | tf_op jit(solution)/shard_map/all_to_all | solution.py:39
Sparse Core Ops, SparseCore 0:
  63.4 81.0 all-gather.1
  154.5 96.2 reduce-scatter.1
where the time goes:
time: 308 us; the launch traced here: 307 us
  waiting for transfers between devices  209 us (68%)
  blocking collectives  49.6 us (16%)
  starting transfers between devices  15 us (5%)
  between operations  13.5 us (4%)
  matrix products  11.9 us (4%)
  local copies, waits for them, and re-layouts  4.76 us (2%)
  other arithmetic  3.48 us (1%)
    reduce_scatter x1, waiting for transfers between devices, local(): lax.psum_scatter(partial_value, 'narrow', scatter_dimension=1, tiled=True)  96.4 us
    all_gather x1, waiting for transfers between devices, local(): slot_rows = lax.all_gather(received, 'narrow', axis=1, tiled=True)  81.2 us
    all_to_all x1, blocking collectives, local(): lax.all_to_all(outgoing, 'wide', split_axis=0, concat_axis=0, tiled=True)  49.6 us
    all_to_all x1, waiting for transfers between devices, local(): lax.all_to_all(summed, 'wide', split_axis=0, concat_axis=0, tiled=True)  31.3 us
    all_to_all x1, starting transfers between devices, local(): lax.all_to_all(summed, 'wide', split_axis=0, concat_axis=0, tiled=True)  14.9 us
    dot_general x1, matrix products, local(): jnp.einsum('sf,fd->sd', hidden, w_down[0], preferred_element_type=jnp.flo...  6.47 us
  transfers between devices with their start and end apart: 3, of which 3 were waited for; matrix products, arithmetic and copies ran while one was open for 0% of the time, Pallas kernels for 0%

commit v1 on v0

--- a/solution.py
+++ b/solution.py
@@ -28,7 +28,9 @@
         jnp.bfloat16
     )
     received = lax.all_to_all(outgoing, "wide", split_axis=0, concat_axis=0, tiled=True)
-    slot_rows = lax.all_gather(received, "narrow", axis=1, tiled=True)
+    slot_rows = jnp.concatenate(
+        lax.all_to_all(jnp.stack([received] * lax.axis_size("narrow")), "narrow", 0, 0), axis=1
+    )
     gate_proj = jnp.einsum("sd,fd->sf", slot_rows, w_gate[0], preferred_element_type=jnp.float32)
     up_proj = jnp.einsum("sd,fd->sf", slot_rows, w_up[0], preferred_element_type=jnp.float32)
     hidden = (jax.nn.silu(gate_proj) * up_proj).astype(jnp.bfloat16)

time: 308 us -> 267 us (0.87)
  waiting for transfers between devices: 209 us -> 118 us
  blocking collectives: 49.6 us -> 101 us
  matrix products: 11.9 us -> 8.78 us
    all_gather x1 -> x0, waiting for transfers between devices: 81.2 us -> none  [local(): slot_rows = lax.all_gather(received, 'narrow', axis=1, tiled=True)]
    all_to_all x0 -> x1, blocking collectives: none -> 51.2 us  [local(): lax.all_to_all(jnp.stack([received] * lax.axis_size('narrow')), 'narrow',...]
    reduce_scatter x1, waiting for transfers between devices: 96.4 us -> 86.9 us  [local(): lax.psum_scatter(partial_value, 'narrow', scatter_dimension=1, tiled=True)]
  transfers between devices with their start and end apart: 3 -> 2, of which waited for: 3 -> 2; matrix products, arithmetic and copies ran while one was open for 0% -> 0% of each run, Pallas kernels for 0% -> 0%
where the time goes in v1:
time: 267 us; the launch traced here: 266 us
  waiting for transfers between devices  118 us (44%)
  blocking collectives  101 us (38%)
  starting transfers between devices  14.9 us (6%)
  between operations  13.5 us (5%)
  matrix products  8.78 us (3%)
  local copies, waits for them, and re-layouts  6.5 us (2%)
  other arithmetic  3.48 us (1%)
    reduce_scatter x1, waiting for transfers between devices, local(): lax.psum_scatter(partial_value, 'narrow', scatter_dimension=1, tiled=True)  86.9 us
    all_to_all x1, blocking collectives, local(): lax.all_to_all(jnp.stack([received] * lax.axis_size('narrow')), 'narrow',...  51.2 us
    all_to_all x1, blocking collectives, local(): lax.all_to_all(outgoing, 'wide', split_axis=0, concat_axis=0, tiled=True)  49.6 us
    all_to_all x1, waiting for transfers between devices, local(): lax.all_to_all(summed, 'wide', split_axis=0, concat_axis=0, tiled=True)  31.3 us
    all_to_all x1, starting transfers between devices, local(): lax.all_to_all(summed, 'wide', split_axis=0, concat_axis=0, tiled=True)  14.9 us
    dot_general x1, matrix products, local(): jnp.einsum('sf,fd->sd', hidden, w_down[0], preferred_element_type=jnp.flo...  5.82 us
  transfers between devices with their start and end apart: 2, of which 2 were waited for; matrix products, arithmetic and copies ran while one was open for 0% of the time, Pallas kernels for 0%

profile of v1, /device:TPU:1, one launch (start us, length us, event | category | flops | bytes accessed | tf_op | source)
XLA Modules:
  0.0 266.4 jit_solution(10591090996789409102)
XLA Ops:
  6.5 0.0 copy-start
  6.5 0.0 reduce-scatter.2.cloned.1.call-start
  6.5 0.9 copy.23
  7.4 0.1 eq.42
  7.5 0.1 eq.38
  7.7 1.8 reduce-window.6
  9.5 0.3 slice_reduce_fusion
  9.8 0.1 fusion.15
  10.0 0.1 sub.7
  10.1 0.1 copy.26
  10.2 0.7 multiply_add_fusion
  10.9 0.4 fusion
  11.3 1.2 convolution_convert_fusion.1
  12.5 0.1 all_to_all.17
  12.6 49.6 %all_to_all.26 = bf16[64,14,256]{2,1,0:T(8,128)(2,1)S(1)} all-to-all(bf16[64,14,256]{2,1,0:T(8,128)(2,1)S(1)} %all_to_all.17), channel_id=1, replica_groups=mesh['wide'=64,'narrow'=8] {'wide'}, dimensions={0} | all-to-all | bytes 917504 | tf_op jit(solution)/shard_map/all_to_all | solution.py:30
  62.3 0.1 stack.4
  62.4 0.2 copy.27
  62.7 0.5 stack.5
  63.1 0.0 copy-start.2
  63.2 51.2 %all_to_all.27 = bf16[8,896,256]{1,2,0:T(8,128)(2,1)S(1)} all-to-all(bf16[8,896,256]{1,2,0:T(8,128)(2,1)S(1)} %stack.5), channel_id=1, replica_groups=mesh['wide'=64,'narrow'=8] {'narrow'}, dimensions={0} | all-to-all | bytes 7340032 | tf_op jit(solution)/shard_map/all_to_all | solution.py:32
  114.4 1.8 copy-done.1
  116.2 0.0 copy-done.2
  116.2 0.9 fusion.5
  117.2 5.8 %convolution_convert_fusion = bf16[896,2048]{1,0:T(8,128)(2,1)} fusion(bf16[896,2048]{0,1:T(8,128)(2,1)} %bitcast.36, bf16[1,176,2048]{2,1,0:T(8,128)(2,1)S(1)} %copy-done, bf16[1,176,2048]{2,1,0:T(8,128)(2,1)S(1)} %copy-done.4, f32[896,176]{0,1:T(8,128)S(1)} %fusion.5), kind=kOutput, calls=%fused_computation | convolution fusion | flops 1294626816 | bytes 9412608 | tf_op jit(solution)/shard_map/sf,fd->sd/dot_general | solution.py:37
  123.0 0.0 reduce-scatter.2.cloned.1.call-update
  123.0 86.9 %reduce-scatter.2.cloned.1.call-done = bf16[896,256]{1,0:T(8,128)(2,1)} async-done(((bf16[896,2048]{1,0:T(8,128)(2,1)}), bf16[896,256]{1,0:T(8,128)(2,1)}) %reduce-scatter.2.cloned.1.call-update) | async-done | bytes 458768 | tf_op jit(solution)/shard_map/reduce_scatter | solution.py:40
  209.9 1.9 all_to_all.20
  211.9 14.9 %all-to-all-start.2 = ((bf16[64,14,256]{2,1,0:T(8,128)(2,1)}), bf16[64,14,256]{2,1,0:T(8,128)(2,1)S(1)}, u32[]{:S(2)}, u32[]{:S(2)}) async-start(bf16[64,14,256]{2,1,0:T(8,128)(2,1)} %all_to_all.20), calls=%async_computation.3 | async-start | bytes 1048576 | tf_op jit(solution)/shard_map/all_to_all | solution.py:41
  226.9 0.3 select_reduce_fusion
  227.2 31.3 %all-to-all-done.2 = bf16[64,14,256]{2,1,0:T(8,128)(2,1)S(1)} async-done(((bf16[64,14,256]{2,1,0:T(8,128)(2,1)}), bf16[64,14,256]{2,1,0:T(8,128)(2,1)S(1)}, u32[]{:S(2)}, u32[]{:S(2)}) %all-to-all-start.2) | async-done | bytes 458784 | tf_op jit(solution)/shard_map/all_to_all | solution.py:41
  258.5 0.1 all_to_all.22
  258.7 0.9 convolution_convert_fusion.2
  (10 shorter events, 0.1 us)
Async XLA Ops:
  6.5 110.6 %copy-start = (bf16[1,176,2048]{2,1,0:T(8,128)(2,1)S(1)}, bf16[1,176,2048]{2,1,0:T(8,128)(2,1)}, u32[]{:S(2)}) copy-start(bf16[1,176,2048]{2,1,0:T(8,128)(2,1)} %param.11) | copy-start | bytes 2162692
  6.5 203.4 %reduce-scatter.2.cloned.1.call-start = ((), (), s32[]{:S(2)}) async-start(), calls=%async_computation.4 | async-start | bytes 4128768 | tf_op jit(solution)/shard_map/reduce_scatter | solution.py:40
  63.1 53.1 %copy-start.2 = (bf16[1,176,2048]{2,1,0:T(8,128)(2,1)S(1)}, bf16[1,176,2048]{2,1,0:T(8,128)(2,1)}, u32[]{:S(2)}) copy-start(bf16[1,176,2048]{2,1,0:T(8,128)(2,1)} %param.9) | copy-start | bytes 2162692
  114.4 1.8 copy-start.1
  114.4 2.8 %copy-start.4 = (bf16[1,176,2048]{2,1,0:T(8,128)(2,1)S(1)}, bf16[1,176,2048]{2,1,0:T(8,128)(2,1)}, u32[]{:S(2)}) copy-start(bf16[1,176,2048]{2,1,0:T(8,128)(2,1)} %param.10) | copy-start | bytes 2162692
  123.0 103.8 %copy-start.3 = (bf16[128,6]{0,1:T(8,128)(2,1)S(1)}, bf16[128,6]{0,1:T(8,128)(2,1)}, u32[]{:S(2)}) copy-start(bf16[128,6]{0,1:T(8,128)(2,1)} %param.8) | copy-start | bytes 4612
  211.9 46.6 %all-to-all-start.2 = ((bf16[64,14,256]{2,1,0:T(8,128)(2,1)}), bf16[64,14,256]{2,1,0:T(8,128)(2,1)S(1)}, u32[]{:S(2)}, u32[]{:S(2)}) async-start(bf16[64,14,256]{2,1,0:T(8,128)(2,1)} %all_to_all.20), calls=%async_computation.3 | async-start | bytes 1048576 | tf_op jit(solution)/shard_map/all_to_all | solution.py:41
Sparse Core Ops, SparseCore 0:
  123.2 86.7 reduce-scatter.1
